TPU v7x, 32 devices: a whole 2x2x4 slice. The times are simulated.
32 devices in a mesh: rows: 16 (over z, y, x), grid: 2 (over core).
Axes of the slice: x: 2, y: 2, z: 4, core: 2. Of those that a mesh axis runs over, the one named last changes fastest.
Arguments:
- library: bfloat16 [8192, 4096], P('rows', 'grid'), may hold values from -6 to 6
- col_scale: float32 [4096], replicated, may hold values from 0.5 to 2
Outputs:
- updated: float32 [4096, 4096], P('rows', 'grid')
- reflectors: float32 [4096, 64], P('rows')
All inputs are finite; a program needn't handle non-finite values.
Results may differ from a plain program's by a relative error of at most 0.0003.
Values may be sent and summed in bfloat16 or wider, within the bound.
A program may use at most 128 MiB of HBM per device.

v0:
```python
import jax
import jax.numpy as jnp
from jax import lax
from jax.sharding import PartitionSpec as P

PANEL = 64


def broadcast(block, axis, source):
    block = jnp.where(lax.axis_index(axis) == source, block, jnp.zeros_like(block))
    return lax.psum(block, axis)


def reflect_panel(panel):
    size, width = panel.shape
    row_line = jnp.arange(size)
    col_line = jnp.arange(width)
    vectors = jnp.zeros((size, width), jnp.float32)
    factor = jnp.zeros((width, width), jnp.float32)

    def one_step(step, carry):
        work, vectors, factor = carry
        column = jnp.sum(jnp.where(col_line[None, :] == step, work, 0.0), axis=1)
        column = jnp.where(row_line >= step, column, 0.0)
        pivot = jnp.sum(jnp.where(row_line == step, column, 0.0))
        length = jnp.sqrt(jnp.sum(column * column))
        sign_factor = jnp.where(pivot >= 0.0, 1.0, -1.0)
        vector = column + jnp.where(row_line == step, sign_factor * length, 0.0)
        scale = 2.0 / jnp.sum(vector * vector)
        project = jnp.dot(vector, work, precision=lax.Precision.HIGHEST)
        work = work - scale * vector[:, None] * project[None, :]
        coupling = jnp.dot(vector, vectors, precision=lax.Precision.HIGHEST)
        column_t = -scale * jnp.dot(factor, coupling, precision=lax.Precision.HIGHEST)
        column_t = column_t + jnp.where(col_line == step, scale, 0.0)
        factor = jnp.where(col_line[None, :] == step, column_t[:, None], factor)
        vectors = jnp.where(col_line[None, :] == step, vector[:, None], vectors)
        return (work, vectors, factor)

    work, vectors, factor = lax.fori_loop(0, width, one_step, (panel, vectors, factor))
    return (vectors, factor)


def per_device(library, col_scale):
    rows_dev, col_block = library.shape
    count_rows = lax.axis_size("rows")
    count_grid = lax.axis_size("grid")
    columns = col_block * count_grid
    row_block = columns // count_rows
    total = rows_dev * count_rows
    grid_place = lax.axis_index("grid")
    rows_place = lax.axis_index("rows")
    own_scale = lax.dynamic_slice_in_dim(col_scale, grid_place * col_block, col_block)
    whole = lax.all_gather(library, "grid", axis=1, tiled=True)
    product = lax.dot_general(
        whole, library, (((0,), (0,)), ((), ())), preferred_element_type=jnp.float32
    )
    gram = lax.psum_scatter(
        product * (col_scale[:, None] * own_scale[None, :] / total),
        "rows",
        scatter_dimension=0,
        tiled=True,
    )
    head = gram[:, :PANEL]
    head = broadcast(head, "grid", 0)
    panel = lax.all_gather(head, "rows", axis=0, tiled=True)
    vectors, factor = reflect_panel(panel)
    own_vectors = lax.dynamic_slice_in_dim(vectors, rows_place * row_block, row_block, 0)
    partial_cross = jnp.dot(own_vectors.T, gram, precision=lax.Precision.HIGHEST)
    cross = lax.psum(partial_cross, "rows")
    mixed = jnp.dot(factor.T, cross, precision=lax.Precision.HIGHEST)
    updated = gram - jnp.dot(own_vectors, mixed, precision=lax.Precision.HIGHEST)
    return (updated, own_vectors)


def solution(mesh):
    return jax.shard_map(
        per_device,
        mesh=mesh,
        in_specs=(P("rows", "grid"), P()),
        out_specs=(P("rows", "grid"), P("rows", None)),
        check_vma=False,
    )
```

profile of v0, /device:TPU:0, one launch (start us, length us, event | category | flops | bytes accessed | tf_op | source)
XLA Modules:
  0.0 1997.8 jit_solution(2636637013112608751)
XLA Ops:
  8.0 17.9 all-gather.3.cloned.1.call-done
  26.0 17.6 multiply_multiply_fusion
  43.7 684.7 %reduce-scatter.2.cloned.1.call-done = f32[256,2048]{1,0:T(8,128)} async-done(((f32[4096,2048]{1,0:T(8,128)}), f32[256,2048]{1,0:T(8,128)}) %reduce-scatter.2.cloned.1.call-update) | async-done | bytes 2097168 | tf_op jit(solution)/shard_map/reduce_scatter | solution.py:57
  730.0 24.8 %all-reduce.3.cloned.1.call-done = f32[256,64]{1,0:T(8,128)} async-done(((f32[256,64]{1,0:T(8,128)}), f32[256,64]{1,0:T(8,128)}) %all-reduce.3.cloned.1.call-update) | async-done | bytes 65552 | tf_op jit(solution)/shard_map/psum | solution.py:11
  755.2 64.3 %all-gather.5.cloned.1.call-done = f32[4096,64]{1,0:T(8,128)} async-done(((f32[256,64]{1,0:T(8,128)}), f32[4096,64]{1,0:T(8,128)}) %all-gather.5.cloned.1.call-update) | async-done | bytes 1048592 | tf_op jit(solution)/shard_map/all_gather | solution.py:65
  819.4 1055.3 %while.19 = (s32[]{:T(128)}, f32[4096,64]{1,0:T(8,128)}, f32[4096,64]{1,0:T(8,128)}, f32[64,64]{1,0:T(8,128)S(1)}, s32[]{:T(128)}, /*index=5*/f32[]{:T(128)}, f32[]{:T(128)}, f32[]{:T(128)}, f32[]{:T(128)}, s32[]{:T(128)}) while((s32[]{:T(128)}, f32[4096,64]{1,0:T(8,128)}, f32[4096,64]{1,0:T(8,128)}, ...), condition=%wide.region_7.8_spmd.clone.clone, body=%wide.region_2.7_spmd.clone.clone.sunk | while | flops 8245573 | bytes 24332360 | solution.py:39
  827.6 3.9 multiply_subtract_fusion.2
  844.1 3.9 multiply_subtract_fusion.2
  860.6 3.9 multiply_subtract_fusion.2
  877.2 3.9 multiply_subtract_fusion.2
  910.2 3.9 multiply_subtract_fusion.2
  926.7 3.9 multiply_subtract_fusion.2
  943.2 3.9 multiply_subtract_fusion.2
  959.7 3.9 multiply_subtract_fusion.2
  976.3 3.9 multiply_subtract_fusion.2
  992.8 3.9 multiply_subtract_fusion.2
  1009.3 3.9 multiply_subtract_fusion.2
  1025.8 3.9 multiply_subtract_fusion.2
  1042.3 3.9 multiply_subtract_fusion.2
  1058.8 3.9 multiply_subtract_fusion.2
  1075.4 3.9 multiply_subtract_fusion.2
  1091.9 3.9 multiply_subtract_fusion.2
  1108.4 3.9 multiply_subtract_fusion.2
  1124.9 3.9 multiply_subtract_fusion.2
  1141.4 3.9 multiply_subtract_fusion.2
  1157.9 3.9 multiply_subtract_fusion.2
  1174.5 3.9 multiply_subtract_fusion.2
  1191.0 3.9 multiply_subtract_fusion.2
  1224.0 3.9 multiply_subtract_fusion.2
  1240.5 3.9 multiply_subtract_fusion.2
  1257.0 3.9 multiply_subtract_fusion.2
  1273.6 3.9 multiply_subtract_fusion.2
  1290.1 3.9 multiply_subtract_fusion.2
  1306.6 3.9 multiply_subtract_fusion.2
  1323.1 3.9 multiply_subtract_fusion.2
  1339.6 3.9 multiply_subtract_fusion.2
  1356.1 3.9 multiply_subtract_fusion.2
  1372.7 3.9 multiply_subtract_fusion.2
  1389.2 3.9 multiply_subtract_fusion.2
  1405.7 3.9 multiply_subtract_fusion.2
  1422.2 3.9 multiply_subtract_fusion.2
  1438.7 3.9 multiply_subtract_fusion.2
  1455.2 3.9 multiply_subtract_fusion.2
  1471.8 3.9 multiply_subtract_fusion.2
  1488.3 3.9 multiply_subtract_fusion.2
  1504.8 3.9 multiply_subtract_fusion.2
  1537.8 3.9 multiply_subtract_fusion.2
  1879.3 107.1 %all-reduce.5.cloned.1.call-done = f32[64,2048]{1,0:T(8,128)} async-done(((f32[64,2048]{1,0:T(8,128)}), f32[64,2048]{1,0:T(8,128)}) %all-reduce.5.cloned.1.call-update) | async-done | bytes 524304 | tf_op jit(solution)/shard_map/psum | solution.py:69
  (1138 shorter events, 767.4 us)
Async XLA Ops:
  7.2 18.8 copy-start.5
  7.2 18.8 all-gather.3.cloned.1.call-start
  7.9 720.5 %reduce-scatter.2.cloned.1.call-start = ((), (), s32[]{:S(2)}) async-start(), calls=%async_computation.2 | async-start | bytes 35651584 | tf_op jit(solution)/shard_map/reduce_scatter | solution.py:57
  43.6 711.2 %all-reduce.3.cloned.1.call-start = ((), (), s32[]{:S(2)}) async-start(), calls=%async_computation.3 | async-start | bytes 262144 | tf_op jit(solution)/shard_map/psum | solution.py:11
  730.0 89.4 %all-gather.5.cloned.1.call-start = ((), (), s32[]{:S(2)}) async-start(), calls=%async_computation.4 | async-start | bytes 2228224 | tf_op jit(solution)/shard_map/all_gather | solution.py:65
  754.9 1231.5 %all-reduce.5.cloned.1.call-start = ((), (), s32[]{:S(2)}) async-start(), calls=%async_computation.5 | async-start | bytes 1048576 | tf_op jit(solution)/shard_map/psum | solution.py:69
  834.2 8.8 copy-start
  850.7 8.8 copy-start
  867.2 8.8 copy-start
  883.7 8.8 copy-start
  900.3 8.8 copy-start
  916.8 8.8 copy-start
  933.3 8.8 copy-start
  949.8 8.8 copy-start
  966.3 8.8 copy-start
  982.8 8.8 copy-start
  999.4 8.8 copy-start
  1015.9 8.8 copy-start
  1032.4 8.8 copy-start
  1048.9 8.8 copy-start
  1065.4 8.8 copy-start
  1082.0 8.8 copy-start
  1098.5 8.8 copy-start
  1115.0 8.8 copy-start
  1131.5 8.8 copy-start
  1148.0 8.8 copy-start
  1197.6 8.8 copy-start
  1214.1 8.8 copy-start
  1230.6 8.8 copy-start
  1247.1 8.8 copy-start
  1263.6 8.8 copy-start
  1362.7 8.8 copy-start
  1379.3 8.8 copy-start
  1395.8 8.8 copy-start
  1412.3 8.8 copy-start
  1511.4 8.8 copy-start
  1527.9 8.8 copy-start
  1544.4 8.8 copy-start
  1560.9 8.8 copy-start
  1577.5 8.8 copy-start
  1676.6 8.8 copy-start
  1693.1 8.8 copy-start
  1709.6 8.8 copy-start
  1726.1 8.8 copy-start
  1825.2 8.8 copy-start
  1841.7 8.8 copy-start
  1858.2 8.8 copy-start
  1877.1 111.0 %copy-start.6 = (f32[256,64]{0,1:T(8,128)}, f32[256,64]{0,1:T(8,128)S(1)}, u32[]{:S(2)}) copy-start(f32[256,64]{0,1:T(8,128)S(1)} %constant_dynamic-slice_fusion) | copy-start | bytes 196612
  (217 other events, 632.0 us)
Sparse Core Ops, SparseCore 0:
  9.6 16.3 all-gather.2
  43.8 684.5 reduce-scatter.1
  731.3 23.5 all-reduce.2
  757.5 61.8 all-gather.4
  1879.5 106.9 all-reduce.4
where the time goes:
time: 2000 us
  waiting for transfers between devices  900 us (45%)
  other arithmetic  496 us (25%)
  matrix products  290 us (14%)
  local copies, waits for them, and re-layouts  158 us (8%)
  loops' own time  140 us (7%)
    reduce_scatter x1, waiting for transfers between devices, per_device(): lax.psum_scatter(product * (col_scale[:, None] * own_scale[None, :] / tot...  685 us
    sub x64, other arithmetic, one_step(): work = work - scale * vector[:, None] * project[None, :]  250 us
    dot_general x64, matrix products, one_step(): coupling = jnp.dot(vector, vectors, precision=lax.Precision.HIGHEST)  184 us
    while x512, local copies, waits for them, and re-layouts  156 us
    reduce_sum x64, other arithmetic, one_step(): column = jnp.sum(jnp.where(col_line[None, :] == step, work, 0.0), axis=1)  150 us
    another operation x1, loops' own time, reflect_panel(): lax.fori_loop(0, width, one_step, (panel, vectors, factor))  140 us
    psum x1, waiting for transfers between devices, per_device(): cross = lax.psum(partial_cross, 'rows')  107 us
    dot_general x64, matrix products, one_step(): project = jnp.dot(vector, work, precision=lax.Precision.HIGHEST)  72.2 us
  transfers between devices with their start and end apart: 5, of which 5 were waited for; matrix products, arithmetic and copies ran while one was open for 0% of the time, Pallas kernels for 0%

commit v1 on v0

--- a/solution.py
+++ b/solution.py
@@ -62,7 +62,12 @@
     )
     head = gram[:, :PANEL]
     head = broadcast(head, "grid", 0)
-    panel = lax.all_gather(head, "rows", axis=0, tiled=True)
+    ring = [head]
+    for hop in range(15):
+        ring.append(lax.ppermute(ring[-1], "rows", [(dev, (dev + 1) % 16) for dev in range(16)]))
+    panel = jnp.roll(
+        jnp.concatenate(ring[::-1], axis=0), (lax.axis_index("rows") + 1) * ring[0].shape[0], axis=0
+    )
     vectors, factor = reflect_panel(panel)
     own_vectors = lax.dynamic_slice_in_dim(vectors, rows_place * row_block, row_block, 0)
     partial_cross = jnp.dot(own_vectors.T, gram, precision=lax.Precision.HIGHEST)

time: 2000 us -> 1870 us (0.935)
  other arithmetic: 496 us -> 384 us
  local copies, waits for them, and re-layouts: 158 us -> 89 us
  waiting for transfers between devices: 900 us -> 961 us
    ppermute x0 -> x15, waiting for transfers between devices: none -> 130 us  [per_device(): lax.ppermute(ring[-1], 'rows', [(dev, (dev + 1) % 16) for dev in range(16)])]
    reduce_sum x64, other arithmetic: 150 us -> 39 us  [one_step(): column = jnp.sum(jnp.where(col_line[None, :] == step, work, 0.0), axis=1)]
    while x512 -> x256, local copies, waits for them, and re-layouts: 156 us -> 84.5 us
    all_gather x1 -> x0, waiting for transfers between devices: 64.3 us -> none  [per_device(): panel = lax.all_gather(head, 'rows', axis=0, tiled=True)]
  transfers between devices with their start and end apart: 5 -> 19, of which waited for: 5 -> 19; matrix products, arithmetic and copies ran while one was open for 0% -> 0% of each run, Pallas kernels for 0% -> 0%
where the time goes in v1:
time: 1870 us
  waiting for transfers between devices  961 us (51%)
  other arithmetic  384 us (21%)
  matrix products  290 us (16%)
  loops' own time  130 us (7%)
  local copies, waits for them, and re-layouts  89 us (5%)
    reduce_scatter x1, waiting for transfers between devices, per_device(): lax.psum_scatter(product * (col_scale[:, None] * own_scale[None, :] / tot...  685 us
    sub x64, other arithmetic, one_step(): work = work - scale * vector[:, None] * project[None, :]  250 us
    dot_general x64, matrix products, one_step(): coupling = jnp.dot(vector, vectors, precision=lax.Precision.HIGHEST)  184 us
    another operation x1, loops' own time, reflect_panel(): lax.fori_loop(0, width, one_step, (panel, vectors, factor))  130 us
    ppermute x15, waiting for transfers between devices, per_device(): lax.ppermute(ring[-1], 'rows', [(dev, (dev + 1) % 16) for dev in range(16)])  130 us
    psum x1, waiting for transfers between devices, per_device(): cross = lax.psum(partial_cross, 'rows')  104 us
    while x256, local copies, waits for them, and re-layouts  84.5 us
    dot_general x64, matrix products, one_step(): project = jnp.dot(vector, work, precision=lax.Precision.HIGHEST)  72.4 us
  transfers between devices with their start and end apart: 19, of which 19 were waited for; matrix products, arithmetic and copies ran while one was open for 0% of the time, Pallas kernels for 0%

profile of v1, /device:TPU:0, one launch (start us, length us, event | category | flops | bytes accessed | tf_op | source)
XLA Modules:
  0.0 1869.8 jit_solution(5926738538869365641)
XLA Ops:
  8.7 17.3 all-gather.2.cloned.1.call-done
  25.9 17.9 multiply_multiply_fusion
  43.9 684.7 %reduce-scatter.2.cloned.1.call-done = f32[256,2048]{1,0:T(8,128)} async-done(((f32[4096,2048]{1,0:T(8,128)}), f32[256,2048]{1,0:T(8,128)}) %reduce-scatter.2.cloned.1.call-update) | async-done | bytes 2097168 | tf_op jit(solution)/shard_map/reduce_scatter | solution.py:57
  730.3 24.8 %all-reduce.3.cloned.1.call-done = f32[256,64]{1,0:T(8,128)} async-done(((f32[256,64]{1,0:T(8,128)}), f32[256,64]{1,0:T(8,128)}) %all-reduce.3.cloned.1.call-update) | async-done | bytes 65552 | tf_op jit(solution)/shard_map/psum | solution.py:11
  756.8 7.9 collective-permute-done
  764.7 8.6 collective-permute-done.1
  773.4 8.6 collective-permute-done.2
  781.9 8.6 collective-permute-done.3
  790.5 8.6 collective-permute-done.4
  799.1 8.6 collective-permute-done.5
  807.6 9.4 collective-permute-done.6
  817.1 9.3 collective-permute-done.7
  826.4 8.6 collective-permute-done.8
  835.0 8.6 collective-permute-done.9
  843.6 8.6 collective-permute-done.10
  852.1 8.6 collective-permute-done.11
  860.7 8.6 collective-permute-done.12
  869.2 8.6 collective-permute-done.13
  877.8 8.6 collective-permute-done.14
  888.1 861.4 %while.19 = (s32[]{:T(128)}, f32[4096,64]{1,0:T(8,128)S(1)}, f32[4096,64]{1,0:T(8,128)}, f32[64,64]{1,0:T(8,128)S(1)}, s32[]{:T(128)}, /*index=5*/f32[]{:T(128)}, f32[]{:T(128)}, f32[]{:T(128)}, f32[]{:T(128)}, s32[]{:T(128)}) while((s32[]{:T(128)}, f32[4096,64]{1,0:T(8,128)S(1)}, f32[4096,64]{1,0:T(8,128)}, ...), condition=%wide.region_7.8_spmd.clone.clone, body=%wide.region_2.7_spmd.clone.clone.sunk | while | flops 8245573 | bytes 15943700 | solution.py:39
  894.3 3.9 multiply_subtract_fusion.2
  907.8 3.9 multiply_subtract_fusion.2
  921.3 3.9 multiply_subtract_fusion.2
  934.8 3.9 multiply_subtract_fusion.2
  948.3 3.9 multiply_subtract_fusion.2
  961.8 3.9 multiply_subtract_fusion.2
  975.3 3.9 multiply_subtract_fusion.2
  988.7 3.9 multiply_subtract_fusion.2
  1002.2 3.9 multiply_subtract_fusion.2
  1015.7 3.9 multiply_subtract_fusion.2
  1029.2 3.9 multiply_subtract_fusion.2
  1056.2 3.9 multiply_subtract_fusion.2
  1069.7 3.9 multiply_subtract_fusion.2
  1083.1 3.9 multiply_subtract_fusion.2
  1096.6 3.9 multiply_subtract_fusion.2
  1110.1 3.9 multiply_subtract_fusion.2
  1123.6 3.9 multiply_subtract_fusion.2
  1137.1 3.9 multiply_subtract_fusion.2
  1150.6 3.9 multiply_subtract_fusion.2
  1164.1 3.9 multiply_subtract_fusion.2
  1177.5 3.9 multiply_subtract_fusion.2
  1191.0 3.9 multiply_subtract_fusion.2
  1204.5 3.9 multiply_subtract_fusion.2
  1218.0 3.9 multiply_subtract_fusion.2
  1231.5 3.9 multiply_subtract_fusion.2
  1245.0 3.9 multiply_subtract_fusion.2
  1258.5 3.9 multiply_subtract_fusion.2
  1754.0 104.3 %all-reduce.5.cloned.1.call-done = f32[64,2048]{1,0:T(8,128)} async-done(((f32[64,2048]{1,0:T(8,128)}), f32[64,2048]{1,0:T(8,128)}) %all-reduce.5.cloned.1.call-update) | async-done | bytes 524304 | tf_op jit(solution)/shard_map/psum | solution.py:74
  (940 shorter events, 641.9 us)
Async XLA Ops:
  7.2 18.8 %all-gather.2.cloned.1.call-start = ((), (), s32[]{:S(2)}) async-start(), calls=%async_computation.1 | async-start | bytes 6291456 | tf_op jit(solution)/shard_map/all_gather | solution.py:53
  7.9 720.7 %reduce-scatter.2.cloned.1.call-start = ((), (), s32[]{:S(2)}) async-start(), calls=%async_computation.2 | async-start | bytes 35651584 | tf_op jit(solution)/shard_map/reduce_scatter | solution.py:57
  43.9 711.2 %all-reduce.3.cloned.1.call-start = ((), (), s32[]{:S(2)}) async-start(), calls=%async_computation.3 | async-start | bytes 262144 | tf_op jit(solution)/shard_map/psum | solution.py:11
  730.2 1128.2 %all-reduce.5.cloned.1.call-start = ((), (), s32[]{:S(2)}) async-start(), calls=%async_computation.4 | async-start | bytes 1048576 | tf_op jit(solution)/shard_map/psum | solution.py:74
  755.1 132.8 %copy-start.4 = (f32[256,64]{1,0:T(8,128)S(1)}, f32[256,64]{1,0:T(8,128)}, u32[]{:S(2)}) copy-start(f32[256,64]{1,0:T(8,128)} %all-reduce.3.cloned.1.call-done) | copy-start | bytes 196612
  755.1 9.6 collective-permute-start
  764.7 8.6 collective-permute-start.1
  773.4 8.6 collective-permute-start.2
  781.9 8.6 collective-permute-start.3
  790.5 8.6 collective-permute-start.4
  799.1 8.6 collective-permute-start.5
  807.6 9.4 collective-permute-start.6
  817.1 9.4 collective-permute-start.7
  826.4 8.6 collective-permute-start.8
  835.0 8.6 collective-permute-start.9
  843.6 8.6 collective-permute-start.10
  852.1 8.6 collective-permute-start.11
  860.7 8.6 collective-permute-start.12
  869.2 8.6 collective-permute-start.13
  877.8 8.6 collective-permute-start.14
  903.8 4.0 copy-start
  917.3 4.0 copy-start
  930.7 4.0 copy-start
  944.2 4.0 copy-start
  957.7 4.0 copy-start
  971.2 4.0 copy-start
  984.7 4.0 copy-start
  998.2 4.0 copy-start
  1011.7 4.0 copy-start
  1025.2 4.0 copy-start
  1038.6 4.0 copy-start
  1052.1 4.0 copy-start
  1065.6 4.0 copy-start
  1079.1 4.0 copy-start
  1106.1 4.0 copy-start
  1173.5 4.0 copy-start
  1227.4 4.0 copy-start
  1240.9 4.0 copy-start
  1294.9 4.0 copy-start
  1362.3 4.0 copy-start
  1429.7 4.0 copy-start
  1483.7 4.0 copy-start
  1497.2 4.0 copy-start
  1551.1 4.0 copy-start
  1618.5 4.0 copy-start
  1686.0 4.0 copy-start
  1739.9 4.0 copy-start
  1751.8 111.4 %copy-start.3 = (f32[256,64]{0,1:T(8,128)}, f32[256,64]{0,1:T(8,128)S(1)}, u32[]{:S(2)}) copy-start(f32[256,64]{0,1:T(8,128)S(1)} %constant_dynamic-slice_fusion) | copy-start | bytes 196612
  (102 other events, 234.8 us)
Sparse Core Ops, SparseCore 0:
  9.5 16.3 all-gather.1
  44.0 684.6 reduce-scatter.1
  731.5 23.5 all-reduce.2
  1754.2 104.1 all-reduce.4
